TPU v7x, 32 devices: a whole 2x2x4 slice. The times are simulated.
32 devices in a mesh: expert: 16 (over z, y, x), etp: 2 (over core).
Axes of the slice: x: 2, y: 2, z: 4, core: 2. Of those that a mesh axis runs over, the one named last changes fastest.
Arguments:
- grad_out: bfloat16 [2048, 3584], P('expert', 'etp'), may hold values from -6 to 6
- combine: bfloat16 [2048, 8], P('expert'), may hold values from 0.099609375 to 2.5
- expert_ids: int32 [2048, 8], P('expert'), may hold values from 0 to 31, all different within a row; in each aligned block of 128 rows (0 to 127, 128 to 255, ...) at most 64 rows name the same one
- saved_gate: bfloat16 [1024, 32, 1024], P(None, 'expert', 'etp'), may hold values from -6 to 6
- saved_up: bfloat16 [1024, 32, 1024], P(None, 'expert', 'etp'), may hold values from -1.5 to 1.5
- gate_weight: bfloat16 [32, 3584, 1024], P('expert', None, 'etp'), may hold values from -0.09375 to 0.09375
- up_weight: bfloat16 [32, 3584, 1024], P('expert', None, 'etp'), may hold values from -0.09375 to 0.09375
- down_weight: bfloat16 [32, 1024, 3584], P('expert', 'etp'), may hold values from -0.09375 to 0.09375
Outputs:
- grad_tokens: bfloat16 [2048, 3584], P('expert', 'etp')
- grad_combine: bfloat16 [2048, 8], P('expert')
Inputs may be any that keep to these rules, and one draw needn't show every extreme that they name: `expert_ids`: each token names 8 different experts. Among the 128 tokens of one block (one index of expert), at most 64 name any one expert, and some blocks reach that bound.
All inputs are finite; a program needn't handle non-finite values.
Results may differ from a plain program's by a relative error of at most 0.012.
Values may be sent and summed in bfloat16 or wider, within the bound.
A program may use at most 192 MiB of HBM per device.

v0:
```python
import jax
import jax.numpy as jnp
from jax import lax
from jax.sharding import PartitionSpec as P


def slot_layout(expert_ids, groups, per_group, capacity):
    token_count, top_count = expert_ids.shape
    experts = groups * per_group
    matches = expert_ids[:, :, None] == jnp.arange(experts, dtype=jnp.int32)[None, None, :]
    expert_loads = jnp.sum(matches.astype(jnp.int32), axis=1)
    earlier = jnp.cumsum(expert_loads, axis=0) - expert_loads
    position = jnp.sum(jnp.where(matches, earlier[:, None, :], 0), axis=2)
    target = expert_ids // per_group
    local_slot = expert_ids % per_group
    flat_slot = (target * capacity + position) * per_group + local_slot
    slot_total = groups * capacity * per_group
    slot_owner = jnp.full((slot_total,), token_count * top_count, jnp.int32)
    slot_owner = slot_owner.at[flat_slot.reshape(-1)].set(
        jnp.arange(token_count * top_count, dtype=jnp.int32)
    )
    return (flat_slot, slot_owner)


def on_device(
    grad_out, combine, expert_ids, saved_gate, saved_up, gate_weight, up_weight, down_weight
):
    groups = lax.axis_size("expert")
    per_group = gate_weight.shape[0]
    half_width = grad_out.shape[1]
    token_count, top_count = expert_ids.shape
    capacity = saved_gate.shape[0] // groups
    slot_rows_count = groups * capacity
    flat_slot, slot_owner = slot_layout(expert_ids, groups, per_group, capacity)
    source_token = slot_owner // top_count
    weight_flat = jnp.concatenate([combine.reshape(-1), jnp.zeros((1,), jnp.bfloat16)])
    slot_weight = jnp.take(weight_flat, slot_owner, axis=0).reshape(groups, capacity, per_group)
    padded = jnp.concatenate([grad_out, jnp.zeros((1, half_width), jnp.bfloat16)], axis=0)
    outgoing = jnp.take(padded, source_token, axis=0).reshape(
        groups, capacity, per_group, half_width
    )
    arrived, arrived_weight = (
        lax.all_to_all(outgoing, "expert", split_axis=0, concat_axis=0, tiled=True),
        lax.all_to_all(slot_weight, "expert", split_axis=0, concat_axis=0, tiled=True),
    )
    slot_rows = lax.all_gather(
        arrived.reshape(slot_rows_count, per_group, half_width), "etp", axis=2, tiled=True
    )
    grad_hidden = jnp.einsum(
        "rld,lfd->rlf", slot_rows, down_weight, preferred_element_type=jnp.float32
    )
    gate_value = saved_gate.astype(jnp.float32)
    up_value = saved_up.astype(jnp.float32)
    gate_sigmoid = jax.nn.sigmoid(gate_value)
    activated = gate_value * gate_sigmoid
    weight_part = jnp.sum(grad_hidden * activated * up_value, axis=2)
    scaled = arrived_weight.reshape(slot_rows_count, per_group, 1).astype(jnp.float32) * grad_hidden
    grad_gate = (
        scaled * up_value * gate_sigmoid * (1.0 + gate_value * (1.0 - gate_sigmoid))
    ).astype(jnp.bfloat16)
    grad_up = (scaled * activated).astype(jnp.bfloat16)
    partial_value = jnp.einsum(
        "rlf,ldf->rld", grad_gate, gate_weight, preferred_element_type=jnp.float32
    )
    partial_value = partial_value + jnp.einsum(
        "rlf,ldf->rld", grad_up, up_weight, preferred_element_type=jnp.float32
    )
    summed, weight_sum = (
        lax.psum(partial_value.astype(jnp.bfloat16), "etp").astype(jnp.float32),
        lax.psum(weight_part.astype(jnp.bfloat16), "etp").astype(jnp.float32),
    )
    slot_grad = lax.dynamic_slice_in_dim(summed, lax.axis_index("etp") * half_width, half_width, 2)
    slot_grad = slot_grad.astype(jnp.bfloat16).reshape(groups, capacity, per_group, half_width)
    slot_dw = weight_sum.astype(jnp.bfloat16).reshape(groups, capacity, per_group)
    returned, returned_weight = (
        lax.all_to_all(slot_grad, "expert", split_axis=0, concat_axis=0, tiled=True),
        lax.all_to_all(slot_dw, "expert", split_axis=0, concat_axis=0, tiled=True),
    )
    gathered = jnp.take(returned.reshape(-1, half_width), flat_slot, axis=0)
    grad_tokens = jnp.sum(gathered.astype(jnp.float32), axis=1).astype(jnp.bfloat16)
    grad_combine = jnp.take(returned_weight.reshape(-1), flat_slot, axis=0)
    return (grad_tokens, grad_combine)


def solution(mesh):
    in_specs = (
        P("expert", "etp"),
        P("expert", None),
        P("expert", None),
        P(None, "expert", "etp"),
        P(None, "expert", "etp"),
        P("expert", None, "etp"),
        P("expert", None, "etp"),
        P("expert", "etp", None),
    )
    out_specs = (P("expert", "etp"), P("expert", None))
    return jax.shard_map(
        on_device, mesh=mesh, in_specs=in_specs, out_specs=out_specs, check_vma=False
    )
```

profile of v0, /device:TPU:28, one launch (start us, length us, event | category | flops | bytes accessed | tf_op | source)
XLA Modules:
  0.0 594.2 jit_solution(13059933077309265864)
XLA Ops:
  7.2 0.7 convert_reduce_fusion
  7.9 0.1 copy.93
  8.0 0.2 reduce_window_sum.11
  8.3 0.7 select_reduce_fusion
  9.0 0.7 compare_select_fusion.2
  9.7 0.1 copy.97
  9.8 0.1 reshape.100
  9.9 4.3 scatter_custom_fusion
  14.3 1.1 concatenate.7
  15.3 10.6 %gather_fusion.1 = bf16[2048,1792]{1,0:T(8,128)(2,1)} fusion(bf16[129,1792]{1,0:T(8,128)(2,1)S(1)} %concatenate.7, s32[2048]{0:T(1024)S(1)} %get-tuple-element.13), kind=kCustom, calls=%fused_computation.1 | custom fusion | bytes 14688256 | tf_op jit(solution)/shard_map/jit(_take)/gather | solution.py:39
  26.0 15.0 %gather.20 = bf16[16,64,2,1792]{3,2,1,0:T(2,128)(2,1)} reshape(bf16[2048,1792]{1,0:T(8,128)(2,1)} %gather_fusion.1) | data formatting | bytes 14680064 | tf_op jit(solution)/shard_map/jit(_take)/gather | solution.py:39
  41.0 0.5 broadcast_in_dim.66
  41.5 0.2 copy.101
  41.8 4.9 copy_select_fusion
  46.7 165.8 %all_to_all.20 = bf16[16,64,2,1792]{3,1,2,0:T(8,128)(2,1)S(1)} all-to-all(bf16[16,64,2,1792]{3,1,2,0:T(8,128)(2,1)S(1)} %copy_select_fusion), channel_id=1, replica_groups=mesh['expert'=16,'etp'=2] {'expert'}, dimensions={0} | all-to-all | bytes 14680064 | tf_op jit(solution)/shard_map/all_to_all | solution.py:43
  212.5 3.8 copy.103
  216.3 0.7 copy-done.2
  216.9 0.1 copy.98
  217.0 0.1 reshape.101
  217.2 13.1 %gather_fusion = bf16[2048]{0:T(1024)(128)(2,1)S(1)} fusion(bf16[1025]{0:T(1024)(128)(2,1)S(1)} %pad_maximum_fusion, s32[2048]{0:T(1024)S(1)} %get-tuple-element.12), kind=kCustom, calls=%fused_computation | custom fusion | bytes 16384 | tf_op jit(solution)/shard_map/jit(_take)/gather | solution.py:37
  230.3 0.5 select_n.76
  230.8 0.8 copy.99
  231.6 6.0 %all-to-all-start = ((bf16[16,64,2]{1,2,0:T(2,128)(2,1)}), bf16[16,64,2]{1,2,0:T(2,128)(2,1)S(1)}, u32[]{:S(2)}, u32[]{:S(2)}) async-start(bf16[16,64,2]{1,2,0:T(2,128)(2,1)} %copy.99), calls=%async_computation | async-start | bytes 16384 | tf_op jit(solution)/shard_map/all_to_all | solution.py:44
  237.6 0.2 all-reduce.3.cloned.1.call-start
  237.8 4.7 copy.105
  242.6 6.3 %copy.104 = bf16[1024,2,512]{0,2,1:T(8,128)(2,1)} copy(bf16[1024,2,512]{2,1,0:T(2,128)(2,1)} %param.12) | data formatting | bytes 4194304 | tf_op args[4]
  249.0 15.4 %fusion.4 = (bf16[1024,2]{0,1:T(2,128)(2,1)S(1)}, f32[2,1024,512]{1,2,0:T(8,128)}) fusion(bf16[1024,2,512]{0,2,1:T(8,128)(2,1)} %copy.104, bf16[1024,2,512]{0,2,1:T(8,128)(2,1)S(1)} %copy-done.1, bf16[1024,2,3584]{2,0,1:T(8,128)(2,1)} %all-gather.2.cloned.1.call-done, bf16[2,512,3584]{2,1,0:T(8,128)(2,1)} %param.15), kind=kOutput, calls=%fused_computation.17 | convolution fusion | flops 7525627904 | bytes 30412800 | tf_op jit(solution)/shard_map/rld,lfd->rlf/dot_general | solution.py:49
  264.4 18.9 %fusion.10 = f32[2,1024,3584]{2,1,0:T(8,128)} fusion(bf16[2,3584,512]{2,1,0:T(8,128)(2,1)} %param.13, bf16[1024,2,512]{0,2,1:T(8,128)(2,1)} %copy.104, bf16[1024,2,512]{0,2,1:T(8,128)(2,1)S(1)} %copy-done.1, f32[2,1024,512]{1,2,0:T(8,128)} %get-tuple-element.15, f32[1024,2]{0,1:T(2,128)S(1)} %reshape.107), kind=kOutput, calls=%fused_computation.27 | convolution fusion | flops 7529824256 | bytes 45096960 | tf_op jit(solution)/shard_map/rlf,ldf->rld/dot_general | solution.py:62
  283.3 20.6 %fusion = bf16[1024,2,3584]{2,0,1:T(8,128)(2,1)} fusion(f32[2,1024,3584]{2,1,0:T(8,128)} %fusion.10, bf16[2,3584,512]{2,1,0:T(8,128)(2,1)} %param.14, f32[2,1024,512]{1,2,0:T(8,128)} %get-tuple-element.15, f32[1024,2]{0,1:T(2,128)S(1)} %reshape.107, bf16[1024,2,512]{0,2,1:T(8,128)(2,1)S(1)} %copy-done.1), kind=kOutput, calls=%fused_computation.6 | convolution fusion | flops 7539261440 | bytes 57679872 | tf_op jit(solution)/shard_map/rlf,ldf->rld/dot_general | solution.py:65
  304.0 3.1 psum.15
  307.1 6.9 %all-to-all-start.3 = ((bf16[16,64,2]{1,2,0:T(2,128)(2,1)}), bf16[16,64,2]{1,2,0:T(2,128)(2,1)S(1)}, u32[]{:S(2)}, u32[]{:S(2)}) async-start(bf16[16,64,2]{1,2,0:T(2,128)(2,1)} %psum.15), calls=%async_computation.3 | async-start | bytes 16384 | tf_op jit(solution)/shard_map/all_to_all | solution.py:77
  314.0 45.1 %all-reduce.3.cloned.1.call-done = bf16[1024,2,3584]{2,0,1:T(8,128)(2,1)} async-done(((bf16[1024,2,3584]{2,0,1:T(8,128)(2,1)}), bf16[1024,2,3584]{2,0,1:T(8,128)(2,1)}) %all-reduce.3.cloned.1.call-update) | async-done | bytes 14680080 | tf_op jit(solution)/shard_map/psum | solution.py:69
  359.1 3.6 convert_convert_fusion
  362.6 3.8 copy.108
  366.5 6.9 %all-to-all-start.2 = ((bf16[16,64,2,1792]{3,1,2,0:T(8,128)(2,1)}), bf16[16,64,2,1792]{3,1,2,0:T(8,128)(2,1)}, u32[]{:S(2)}, u32[]{:S(2)}) async-start(bf16[16,64,2,1792]{3,1,2,0:T(8,128)(2,1)} %copy.108), calls=%async_computation.2 | async-start | bytes 14680064 | tf_op jit(solution)/shard_map/all_to_all | solution.py:76
  373.4 0.1 copy.110
  373.5 0.1 reshape.126
  373.6 0.2 copy.112
  373.8 0.3 reshape.106
  374.2 6.8 %gather_fusion.3 = bf16[1024]{0:T(1024)(128)(2,1)S(1)} fusion(bf16[2048]{0:T(1024)(128)(2,1)S(1)} %reshape.106, s32[1024]{0:T(1024)S(1)} %broadcast_clamp_fusion.1), kind=kCustom, calls=%fused_computation.3 | custom fusion | bytes 8192 | tf_op jit(solution)/shard_map/jit(_take)/gather | solution.py:81
  381.0 0.1 reshape.133
  381.1 0.6 broadcast_select_fusion
  381.7 0.1 copy.96
  381.9 158.7 %all-to-all-done.2 = bf16[16,64,2,1792]{3,1,2,0:T(8,128)(2,1)} async-done(((bf16[16,64,2,1792]{3,1,2,0:T(8,128)(2,1)}), bf16[16,64,2,1792]{3,1,2,0:T(8,128)(2,1)}, u32[]{:S(2)}, u32[]{:S(2)}) %all-to-all-start.2) | async-done | bytes 7340064 | tf_op jit(solution)/shard_map/all_to_all | solution.py:76
  540.5 14.6 %copy.109 = bf16[16,64,2,1792]{3,2,1,0:T(2,128)(2,1)} copy(bf16[16,64,2,1792]{3,1,2,0:T(8,128)(2,1)} %all-to-all-done.2) | data formatting | bytes 14680064 | tf_op jit(solution)/shard_map/all_to_all | solution.py:76
  555.1 15.6 %reshape.104 = bf16[2048,1792]{1,0:T(8,128)(2,1)} reshape(bf16[16,64,2,1792]{3,2,1,0:T(2,128)(2,1)} %copy.109) | data formatting | bytes 14680064 | tf_op jit(solution)/shard_map/reshape | solution.py:79
  570.7 12.0 %gather_fusion.2 = bf16[1024,1792]{1,0:T(8,128)(2,1)} fusion(bf16[2048,1792]{1,0:T(8,128)(2,1)} %reshape.104, s32[1024]{0:T(1024)S(1)} %broadcast_clamp_fusion.1), kind=kCustom, calls=%fused_computation.2 | custom fusion | bytes 7344128 | tf_op jit(solution)/shard_map/jit(_take)/gather | solution.py:79
  582.7 4.7 fusion.9
  (25 shorter events, 0.5 us)
Async XLA Ops:
  7.2 241.8 %all-gather.2.cloned.1.call-start = ((), (), s32[]{:S(2)}) async-start(), calls=%async_computation.4 | async-start | bytes 22020096 | tf_op jit(solution)/shard_map/all_gather | solution.py:46
  216.2 0.7 copy-start.2
  216.9 20.9 %copy-start = (bf16[1024,2,512]{2,1,0:T(2,128)(2,1)S(1)}, bf16[1024,2,512]{2,1,0:T(2,128)(2,1)}, u32[]{:S(2)}) copy-start(bf16[1024,2,512]{2,1,0:T(2,128)(2,1)} %param.11) | copy-start | bytes 6291460
  231.6 17.3 %all-to-all-start = ((bf16[16,64,2]{1,2,0:T(2,128)(2,1)}), bf16[16,64,2]{1,2,0:T(2,128)(2,1)S(1)}, u32[]{:S(2)}, u32[]{:S(2)}) async-start(bf16[16,64,2]{1,2,0:T(2,128)(2,1)} %copy.99), calls=%async_computation | async-start | bytes 16384 | tf_op jit(solution)/shard_map/all_to_all | solution.py:44
  237.6 121.5 %all-reduce.3.cloned.1.call-start = ((), (), s32[]{:S(2)}) async-start(), calls=%async_computation.5 | async-start | bytes 29360128 | tf_op jit(solution)/shard_map/psum | solution.py:69
  242.6 6.4 %copy-start.1 = (bf16[1024,2,512]{0,2,1:T(8,128)(2,1)S(1)}, bf16[1024,2,512]{0,2,1:T(8,128)(2,1)}, u32[]{:S(2)}) copy-start(bf16[1024,2,512]{0,2,1:T(8,128)(2,1)} %copy.105) | copy-start | bytes 6291460
  307.1 59.4 %all-to-all-start.3 = ((bf16[16,64,2]{1,2,0:T(2,128)(2,1)}), bf16[16,64,2]{1,2,0:T(2,128)(2,1)S(1)}, u32[]{:S(2)}, u32[]{:S(2)}) async-start(bf16[16,64,2]{1,2,0:T(2,128)(2,1)} %psum.15), calls=%async_computation.3 | async-start | bytes 16384 | tf_op jit(solution)/shard_map/all_to_all | solution.py:77
  366.5 174.1 %all-to-all-start.2 = ((bf16[16,64,2,1792]{3,1,2,0:T(8,128)(2,1)}), bf16[16,64,2,1792]{3,1,2,0:T(8,128)(2,1)}, u32[]{:S(2)}, u32[]{:S(2)}) async-start(bf16[16,64,2,1792]{3,1,2,0:T(8,128)(2,1)} %copy.108), calls=%async_computation.2 | async-start | bytes 14680064 | tf_op jit(solution)/shard_map/all_to_all | solution.py:76
Sparse Core Ops, SparseCore 0:
  216.4 27.3 all-gather.1
  304.0 55.0 all-reduce.2
where the time goes:
time: 596 us; the launch traced here: 594 us
  waiting for transfers between devices  204 us (34%)
  blocking collectives  169 us (28%)
  local copies, waits for them, and re-layouts  116 us (19%)
  matrix products  54.9 us (9%)
  starting transfers between devices  20.1 us (3%)
  other arithmetic  16.2 us (3%)
  between operations  14.2 us (2%)
    all_to_all x1, blocking collectives, on_device(): lax.all_to_all(outgoing, 'expert', split_axis=0, concat_axis=0, tiled=True)  166 us
    all_to_all x1, waiting for transfers between devices, on_device(): lax.all_to_all(slot_grad, 'expert', split_axis=0, concat_axis=0, tiled=True)  159 us
    psum x1, waiting for transfers between devices, on_device(): lax.psum(partial_value.astype(jnp.bfloat16), 'etp').astype(jnp.float32)  45.1 us
    gather x2, local copies, waits for them, and re-layouts, on_device(): jnp.take(padded, source_token, axis=0)  25.6 us
    dot_general x1, matrix products, on_device(): jnp.einsum('rlf,ldf->rld', grad_up, up_weight, preferred_element_type=jnp...  20.6 us
    dot_general x1, matrix products, on_device(): jnp.einsum('rlf,ldf->rld', grad_gate, gate_weight, preferred_element_type...  18.9 us
    reshape x1, local copies, waits for them, and re-layouts, on_device(): gathered = jnp.take(returned.reshape(-1, half_width), flat_slot, axis=0)  15.6 us
    dot_general x1, matrix products, on_device(): jnp.einsum('rld,lfd->rlf', slot_rows, down_weight, preferred_element_type...  15.4 us
  transfers between devices with their start and end apart: 5, of which 2 were waited for; matrix products, arithmetic and copies ran while one was open for 7% of the time, Pallas kernels for 0%

commit v1 on v0

v1 whole, which is shorter than its diff:
```python
import jax
import jax.numpy as jnp
from jax import lax
from jax.sharding import PartitionSpec as P


def on_device(
    grad_out, combine, expert_ids, saved_gate, saved_up, gate_weight, up_weight, down_weight
):
    groups = lax.axis_size("expert")
    per_group = gate_weight.shape[0]
    tokens = grad_out.shape[0]
    capacity = saved_gate.shape[0] // groups
    hidden = saved_gate.shape[2]
    experts = groups * per_group
    chosen = expert_ids[:, :, None] == jnp.arange(experts, dtype=jnp.int32)[None, None, :]
    weights = jnp.sum(jnp.where(chosen, combine[:, :, None].astype(jnp.float32), 0.0), axis=1)
    weights = weights.astype(jnp.bfloat16).reshape(tokens, groups, per_group)
    weights = lax.all_to_all(
        weights.transpose(1, 2, 0), "expert", split_axis=0, concat_axis=0, tiled=True
    )
    rows = lax.all_gather(grad_out, "expert", axis=0, tiled=True)
    rows = lax.all_gather(rows, "etp", axis=1, tiled=True)
    rows = rows.reshape(groups, tokens, -1)
    named = (weights > 0).astype(jnp.float32)
    position = jnp.cumsum(named, axis=2) - named
    slot = jnp.where(named > 0, position, -1.0)
    select = slot[:, :, None, :] == jnp.arange(capacity, dtype=jnp.float32)[None, None, :, None]
    scale = jnp.sum(jnp.where(select, weights[:, :, None, :].astype(jnp.float32), 0.0), axis=3)
    scale = scale.transpose(1, 0, 2)[..., None]
    select = select.astype(jnp.bfloat16)
    slot_rows = jnp.einsum(
        "blct,btd->lbcd", select, rows, preferred_element_type=jnp.bfloat16
    )
    grad_hidden = jnp.einsum(
        "lbcd,lfd->lbcf", slot_rows, down_weight, preferred_element_type=jnp.float32
    )
    gate_value = saved_gate.reshape(groups, capacity, per_group, hidden).transpose(2, 0, 1, 3)
    up_value = saved_up.reshape(groups, capacity, per_group, hidden).transpose(2, 0, 1, 3)
    gate_value = gate_value.astype(jnp.float32)
    up_value = up_value.astype(jnp.float32)
    gate_sigmoid = jax.nn.sigmoid(gate_value)
    activated = gate_value * gate_sigmoid
    weight_part = jnp.sum(grad_hidden * activated * up_value, axis=3)
    scaled = scale * grad_hidden
    grad_gate = (
        scaled * up_value * gate_sigmoid * (1.0 + gate_value * (1.0 - gate_sigmoid))
    ).astype(jnp.bfloat16)
    grad_up = (scaled * activated).astype(jnp.bfloat16)
    weight_tok = jnp.einsum(
        "blct,lbc->blt", select, weight_part.astype(jnp.bfloat16),
        preferred_element_type=jnp.float32,
    ).astype(jnp.bfloat16)
    weight_tok = lax.psum(weight_tok, "etp")
    weight_tok = lax.all_to_all(weight_tok, "expert", split_axis=0, concat_axis=0, tiled=True)
    weight_tok = weight_tok.transpose(2, 0, 1).reshape(tokens, 1, experts)
    grad_combine = jnp.sum(
        jnp.where(chosen, weight_tok.astype(jnp.float32), 0.0), axis=2
    ).astype(jnp.bfloat16)
    partial = jnp.einsum(
        "lbcf,ldf->lbcd", grad_gate, gate_weight, preferred_element_type=jnp.float32
    )
    partial = partial + jnp.einsum(
        "lbcf,ldf->lbcd", grad_up, up_weight, preferred_element_type=jnp.float32
    )
    partial = jnp.einsum(
        "blct,lbcd->btd", select, partial.astype(jnp.bfloat16),
        preferred_element_type=jnp.float32,
    ).astype(jnp.bfloat16)
    partial = partial.reshape(groups * tokens, -1)
    partial = lax.psum_scatter(partial, "etp", scatter_dimension=1, tiled=True)
    grad_tokens = lax.psum_scatter(partial, "expert", scatter_dimension=0, tiled=True)
    return (grad_tokens, grad_combine)


def solution(mesh):
    in_specs = (
        P("expert", "etp"),
        P("expert", None),
        P("expert", None),
        P(None, "expert", "etp"),
        P(None, "expert", "etp"),
        P("expert", None, "etp"),
        P("expert", None, "etp"),
        P("expert", "etp", None),
    )
    out_specs = (P("expert", "etp"), P("expert", None))
    return jax.shard_map(
        on_device, mesh=mesh, in_specs=in_specs, out_specs=out_specs, check_vma=False
    )
```

time: 596 us -> 414 us (0.69)
  blocking collectives: 169 us -> 18.8 us
  local copies, waits for them, and re-layouts: 116 us -> 6.06 us
  waiting for transfers between devices: 204 us -> 276 us
  matrix products: 54.9 us -> 79.7 us
  starting transfers between devices: 20.1 us -> 6.17 us
    reduce_scatter x0 -> x2, waiting for transfers between devices: none -> 164 us  [the longest x1 141 us: on_device(): lax.psum_scatter(partial, 'expert', scatter_dimension=0, tiled=True)]
    all_to_all x3 -> x1, waiting for transfers between devices: 159 us -> 0.01 us  [on_device(): lax.all_to_all(weights.transpose(1, 2, 0), 'expert', split_axis=0, concat...]
    all_to_all x1, blocking collectives: 166 us -> 16.3 us  [on_device(): lax.all_to_all(weight_tok, 'expert', split_axis=0, concat_axis=0, tiled=T...]
    all_gather x1 -> x2, waiting for transfers between devices: 0.01 us -> 112 us  [the longest x1 105 us: on_device(): rows = lax.all_gather(grad_out, 'expert', axis=0, tiled=True)]
    gather x7 -> x0, local copies, waits for them, and re-layouts: 57.7 us -> none  [the longest x2 25.6 us: on_device(): jnp.take(padded, source_token, axis=0)]
    psum x1 -> x0, waiting for transfers between devices: 45.1 us -> none  [on_device(): lax.psum(partial_value.astype(jnp.bfloat16), 'etp').astype(jnp.float32)]
    dot_general x3 -> x5, matrix products: 54.9 us -> 79.7 us  [the longest x1 25 us: on_device(): jnp.einsum('blct,lbcd->btd', select, partial.astype(jnp.bfloat16), prefer...]
    reshape x7 -> x0, local copies, waits for them, and re-layouts: 20 us -> none  [the longest x1 15.6 us: on_device(): gathered = jnp.take(returned.reshape(-1, half_width), flat_slot, axis=0)]
  transfers between devices with their start and end apart: 5 -> 5, of which waited for: 2 -> 4; matrix products, arithmetic and copies ran while one was open for 7% -> 4% of each run, Pallas kernels for 0% -> 0%
where the time goes in v1:
time: 414 us; the launch traced here: 411 us
  waiting for transfers between devices  276 us (67%)
  matrix products  79.7 us (19%)
  blocking collectives  18.8 us (5%)
  between operations  13.9 us (3%)
  other arithmetic  10.5 us (3%)
  starting transfers between devices  6.17 us (1%)
  local copies, waits for them, and re-layouts  6.06 us (1%)
    reduce_scatter x1, waiting for transfers between devices, on_device(): lax.psum_scatter(partial, 'expert', scatter_dimension=0, tiled=True)  141 us
    all_gather x1, waiting for transfers between devices, on_device(): rows = lax.all_gather(grad_out, 'expert', axis=0, tiled=True)  105 us
    dot_general x1, matrix products, on_device(): jnp.einsum('blct,lbcd->btd', select, partial.astype(jnp.bfloat16), prefer...  25 us
    reduce_scatter x1, waiting for transfers between devices, on_device(): partial = lax.psum_scatter(partial, 'etp', scatter_dimension=1, tiled=True)  22.3 us
    dot_general x1, matrix products, on_device(): jnp.einsum('lbcd,lfd->lbcf', slot_rows, down_weight, preferred_element_ty...  21.5 us
    dot_general x1, matrix products, on_device(): jnp.einsum('lbcf,ldf->lbcd', grad_gate, gate_weight, preferred_element_ty...  16.6 us
    dot_general x1, matrix products, on_device(): jnp.einsum('lbcf,ldf->lbcd', grad_up, up_weight, preferred_element_type=j...  16.4 us
    all_to_all x1, blocking collectives, on_device(): lax.all_to_all(weight_tok, 'expert', split_axis=0, concat_axis=0, tiled=T...  16.3 us
  transfers between devices with their start and end apart: 5, of which 4 were waited for; matrix products, arithmetic and copies ran while one was open for 4% of the time, Pallas kernels for 0%

profile of v1, /device:TPU:28, one launch (start us, length us, event | category | flops | bytes accessed | tf_op | source)
XLA Modules:
  0.0 411.1 jit_solution(12846402701796683711)
XLA Ops:
  7.2 0.0 copy-start.3
  7.2 0.0 copy-start.2
  7.2 0.0 copy-start
  7.2 0.0 all-gather.3.cloned.1.call-start
  7.2 0.7 all-gather.3.cloned.1.call-update
  7.9 0.0 all-gather.5.cloned.1.call-start
  8.0 104.8 %all-gather.3.cloned.1.call-done = bf16[2048,1792]{1,0:T(8,128)(2,1)} async-done(((bf16[128,1792]{1,0:T(8,128)(2,1)}), bf16[2048,1792]{1,0:T(8,128)(2,1)}) %all-gather.3.cloned.1.call-update) | async-done | bytes 7340048 | tf_op jit(solution)/shard_map/all_gather | solution.py:22
  112.8 0.0 all-gather.5.cloned.1.call-update
  112.8 0.0 copy-done.3
  112.8 0.0 copy-done.2
  112.9 0.6 select_reduce_fusion.2
  113.5 6.0 %all-to-all-start = ((bf16[16,2,128]{2,1,0:T(2,128)(2,1)}), bf16[16,2,128]{2,1,0:T(2,128)(2,1)S(1)}, u32[]{:S(2)}, u32[]{:S(2)}) async-start(bf16[16,2,128]{2,1,0:T(2,128)(2,1)} %bitcast.1), calls=%async_computation | async-start | bytes 16384 | tf_op jit(solution)/shard_map/all_to_all | solution.py:19
  119.5 0.0 reduce-scatter.3.cloned.1.call-start
  119.5 0.0 copy-done
  119.6 3.1 copy.40
  122.7 0.0 copy-start.1
  122.7 4.2 %convert_element_type.97 = f32[1024,2,512]{2,1,0:T(2,128)} convert(bf16[1024,2,512]{2,1,0:T(2,128)(2,1)S(1)} %copy-done) | non-fusion elementwise | flops 1048576 | bytes 6291456 | tf_op jit(solution)/shard_map/convert_element_type | solution.py:40
  126.8 0.0 copy-done.1
  126.8 2.9 copy.39
  129.7 3.9 convert_element_type.96
  133.7 0.0 all-to-all-done
  133.7 0.8 reduce_window_sum.11
  134.5 0.4 select_reduce_fusion
  134.9 6.8 %all-gather.5.cloned.1.call-done = bf16[2048,3584]{1,0:T(8,128)(2,1)} async-done(((bf16[2048,1792]{1,0:T(8,128)(2,1)}), bf16[2048,3584]{1,0:T(8,128)(2,1)}) %all-gather.5.cloned.1.call-update) | async-done | bytes 14680080 | tf_op jit(solution)/shard_map/all_gather | solution.py:23
  141.7 21.5 %multiply_convert_fusion = (bf16[2,16,64,512]{3,2,1,0:T(8,128)(2,1)}, bf16[2,16,64,512]{3,2,1,0:T(8,128)(2,1)}, bf16[2,16,64]{2,1,0:T(8,128)(2,1)S(1)}) fusion(f32[2,16,64]{2,1,0:T(8,128)S(1)} %copy.37, f32[1024,2,512]{2,1,0:T(2,128)} %convert_element_type.97, f32[1024,2,512]{2,1,0:T(2,128)} %convert_element_type.96, f32[2,16,64,512]{3,2,1,0:T(8,128)} %bitcast.49, ...), kind=kOutput, calls=%fused_computation.12 | convolution fusion | flops 9417521152 | bytes 43020288 | tf_op jit(solution)/shard_map/lbcd,lfd->lbcf/dot_general | solution.py:35
  163.2 0.0 copy-start.4
  163.2 16.4 %fusion.6 = f32[2,16,64,3584]{3,2,0,1:T(8,128)} fusion(bf16[2,3584,512]{2,1,0:T(8,128)(2,1)} %param.14, bf16[2,16,64,512]{3,2,1,0:T(8,128)(2,1)} %get-tuple-element.2), kind=kOutput, calls=%fused_computation.7 | convolution fusion | flops 7516192768 | bytes 38797312 | tf_op jit(solution)/shard_map/lbcf,ldf->lbcd/dot_general | solution.py:63
  179.6 0.0 copy-done.4
  179.6 16.6 %fusion.8 = f32[2,16,64,3584]{3,2,0,1:T(8,128)} fusion(bf16[2,3584,512]{2,1,0:T(8,128)(2,1)} %param.13, bf16[2,16,64,512]{3,2,1,0:T(8,128)(2,1)S(1)} %copy-done.4), kind=kOutput, calls=%fused_computation.9 | convolution fusion | flops 7516192768 | bytes 38797312 | tf_op jit(solution)/shard_map/lbcf,ldf->lbcd/dot_general | solution.py:60
  196.2 25.0 %bitcast_convert_fusion = bf16[16,128,3584]{2,1,0:T(8,128)(2,1)} fusion(f32[2,16,64,3584]{3,2,0,1:T(8,128)} %fusion.8, f32[2,16,64,3584]{3,2,0,1:T(8,128)} %fusion.6, f32[16,2,128]{2,1,0:T(2,128)S(1)} %copy.36), kind=kOutput, calls=%fused_computation | convolution fusion | flops 1901330432 | bytes 73416704 | tf_op jit(solution)/shard_map/blct,lbcd->btd/dot_general | solution.py:66
  221.2 0.0 reduce-scatter.3.cloned.1.call-update
  221.2 0.0 reduce-scatter.5.cloned.1.call-start
  221.3 22.3 %reduce-scatter.3.cloned.1.call-done = bf16[2048,1792]{1,0:T(8,128)(2,1)} async-done(((bf16[2048,3584]{1,0:T(8,128)(2,1)}), bf16[2048,1792]{1,0:T(8,128)(2,1)}) %reduce-scatter.3.cloned.1.call-update) | async-done | bytes 7340048 | tf_op jit(solution)/shard_map/reduce_scatter | solution.py:71
  243.6 0.0 reduce-scatter.5.cloned.1.call-update
  243.6 0.3 fusion.15
  243.9 2.5 psum.7
  246.4 16.3 %all_to_all.10 = bf16[16,2,128]{2,1,0:T(2,128)(2,1)S(1)} all-to-all(bf16[16,2,128]{2,1,0:T(2,128)(2,1)S(1)} %psum.7), channel_id=1, replica_groups=mesh['expert'=16,'etp'=2] {'expert'}, dimensions={0} | all-to-all | bytes 16384 | tf_op jit(solution)/shard_map/all_to_all | solution.py:55
  262.7 0.6 select_reduce_fusion.1
  263.3 141.2 %reduce-scatter.5.cloned.1.call-done = bf16[128,1792]{1,0:T(8,128)(2,1)} async-done(((bf16[2048,1792]{1,0:T(8,128)(2,1)}), bf16[128,1792]{1,0:T(8,128)(2,1)}) %reduce-scatter.5.cloned.1.call-update) | async-done | bytes 458768 | tf_op jit(solution)/shard_map/reduce_scatter | solution.py:72
  (8 shorter events, 0.1 us)
Async XLA Ops:
  7.2 105.7 %copy-start.3 = (bf16[128,8]{0,1:T(8,128)(2,1)S(1)}, bf16[128,8]{0,1:T(8,128)(2,1)}, u32[]{:S(2)}) copy-start(bf16[128,8]{0,1:T(8,128)(2,1)} %param.9) | copy-start | bytes 6148
  7.2 105.7 %copy-start.2 = (s32[128,8]{0,1:T(8,128)S(1)}, s32[128,8]{0,1:T(8,128)}, u32[]{:S(2)}) copy-start(s32[128,8]{0,1:T(8,128)} %param.10) | copy-start | bytes 12292
  7.2 112.4 %copy-start = (bf16[1024,2,512]{2,1,0:T(2,128)(2,1)S(1)}, bf16[1024,2,512]{2,1,0:T(2,128)(2,1)}, u32[]{:S(2)}) copy-start(bf16[1024,2,512]{2,1,0:T(2,128)(2,1)} %param.11) | copy-start | bytes 6291460
  7.2 105.6 %all-gather.3.cloned.1.call-start = ((), (), s32[]{:S(2)}) async-start(), calls=%async_computation.4 | async-start | bytes 7798784 | tf_op jit(solution)/shard_map/all_gather | solution.py:22
  7.9 133.8 %all-gather.5.cloned.1.call-start = ((), (), s32[]{:S(2)}) async-start(), calls=%async_computation.5 | async-start | bytes 22020096 | tf_op jit(solution)/shard_map/all_gather | solution.py:23
  113.5 20.2 %all-to-all-start = ((bf16[16,2,128]{2,1,0:T(2,128)(2,1)}), bf16[16,2,128]{2,1,0:T(2,128)(2,1)S(1)}, u32[]{:S(2)}, u32[]{:S(2)}) async-start(bf16[16,2,128]{2,1,0:T(2,128)(2,1)} %bitcast.1), calls=%async_computation | async-start | bytes 16384 | tf_op jit(solution)/shard_map/all_to_all | solution.py:19
  119.5 124.1 %reduce-scatter.3.cloned.1.call-start = ((), (), s32[]{:S(2)}) async-start(), calls=%async_computation.6 | async-start | bytes 22020096 | tf_op jit(solution)/shard_map/reduce_scatter | solution.py:71
  122.7 4.2 %copy-start.1 = (bf16[1024,2,512]{2,1,0:T(2,128)(2,1)S(1)}, bf16[1024,2,512]{2,1,0:T(2,128)(2,1)}, u32[]{:S(2)}) copy-start(bf16[1024,2,512]{2,1,0:T(2,128)(2,1)} %param.12) | copy-start | bytes 6291460
  163.2 16.4 %copy-start.4 = (bf16[2,16,64,512]{3,2,1,0:T(8,128)(2,1)S(1)}, bf16[2,16,64,512]{3,2,1,0:T(8,128)(2,1)}, u32[]{:S(2)}) copy-start(bf16[2,16,64,512]{3,2,1,0:T(8,128)(2,1)} %get-tuple-element.3) | copy-start | bytes 6291460
  221.2 183.4 %reduce-scatter.5.cloned.1.call-start = ((), (), s32[]{:S(2)}) async-start(), calls=%async_computation.7 | async-start | bytes 7798784 | tf_op jit(solution)/shard_map/reduce_scatter | solution.py:72
Sparse Core Ops, SparseCore 0:
  10.7 102.0 all-gather.2
  114.4 27.2 all-gather.4
  221.3 22.2 reduce-scatter.2
  246.3 158.2 reduce-scatter.4
